TPU v7x, 256 devices: a whole 4x4x8 slice. The times are simulated.
256 devices in a mesh: pole: 4 (over y), row: 8 (over z_lo, x), col: 8 (over z_hi, core).
Axes of the slice: x: 4, y: 4, z: 8 (z_hi: 4, z_lo: 2; z = z_hi * 2 + z_lo), core: 2. Of those that a mesh axis runs over, the one named last changes fastest.
Arguments:
- found_inverse: bfloat16 [4, 2, 8192, 8, 8, 128], P('pole', None, 'row', None, 'col'), may hold values from -0.125 to 0.125
- l_panel: bfloat16 [4, 2, 8192, 512], P('pole', None, ('row', 'col')), may hold values from -1.5 to 1.5
- block_pattern: int32 [64, 4], P(('row', 'col')), may hold values 0 or 1
- sup_widths: int32 [4], replicated, may hold values from 1 to 128, 320 in all
- diag_inverse: bfloat16 [4, 2, 512, 128], P('pole'), may hold values from -6 to 6
- pole_weights: float32 [4, 2], P('pole'), may hold values from -4 to 4
Outputs:
- density: float32 [512, 8192], P('col', 'row')
- diagonal: float32 [512, 128], replicated
Inputs may be any that keep to these rules, and one draw needn't show every extreme that they name: `sup_widths`: one supernode has exactly 128 columns.
All inputs are finite; a program needn't handle non-finite values. No bound on the sum of `block_pattern` on one device may be relied on, other than what follows from the above.
Results may differ from a plain program's by a relative error of at most 0.0003.
Values may be sent and summed in bfloat16 or wider, within the bound.
A program may use at most 128 MiB of HBM per device.

v0:
```python
import jax
import jax.numpy as jnp
from jax import lax
from jax.sharding import PartitionSpec as P


def contract(left, right):
    return jnp.einsum("jk,ij->ki", left, right, preferred_element_type=jnp.float32)


def pair_product(left, right):
    return jnp.einsum("ika,kbi->kab", left, right, precision=lax.Precision.HIGHEST)


def per_device(found_inverse, l_panel, block_pattern, sup_widths, diag_inverse, pole_weights):
    slot_width = diag_inverse.shape[-1]
    total_cols = l_panel.shape[-1]
    supernodes = total_cols // slot_width
    row_count = lax.axis_size("row")
    row_index = lax.axis_index("row")
    col_index = lax.axis_index("col")
    columns = jnp.arange(total_cols, dtype=jnp.int32)
    column_ok = columns % slot_width < jnp.repeat(sup_widths, slot_width)
    block_ok = jnp.repeat(block_pattern[0], slot_width) == 1
    masked = jnp.where(
        (column_ok & block_ok)[None, None, :], l_panel[0], jnp.zeros((), jnp.bfloat16)
    )
    column_rows = lax.all_gather(masked, "row", axis=1, tiled=True)
    own_rows = lax.all_gather(masked, "col", axis=1, tiled=True)
    local_rows = found_inverse.shape[2]
    inverse = found_inverse[0].reshape(2, local_rows, row_count * slot_width)
    part_real = contract(column_rows[1], inverse[1]) - contract(column_rows[0], inverse[0])
    part_imag = -(contract(column_rows[1], inverse[0]) + contract(column_rows[0], inverse[1]))
    w_real = pole_weights[0, 0]
    w_imag = pole_weights[0, 1]
    weighted = w_real * part_real - w_imag * part_imag
    part = lax.psum_scatter(weighted, "col", scatter_dimension=0, tiled=True)
    density = lax.psum(part, "pole")
    lifted = own_rows.astype(jnp.float32).reshape(2, local_rows, supernodes, slot_width)
    upper_real = part_real.reshape(supernodes, slot_width, local_rows)
    upper_imag = part_imag.reshape(supernodes, slot_width, local_rows)
    t_real = pair_product(lifted[0], upper_real) - pair_product(lifted[1], upper_imag)
    t_imag = pair_product(lifted[0], upper_imag) + pair_product(lifted[1], upper_real)
    lead_flag = ((row_index == 0) & (col_index == 0)).astype(jnp.float32)
    d_real = diag_inverse[0, 0].astype(jnp.float32).reshape(supernodes, slot_width, slot_width)
    d_imag = diag_inverse[0, 1].astype(jnp.float32).reshape(supernodes, slot_width, slot_width)
    local_term = lead_flag * (w_real * d_real - w_imag * d_imag) - (
        w_real * t_real - w_imag * t_imag
    )
    diagonal = lax.psum(local_term.reshape(total_cols, slot_width), ("pole", "row", "col"))
    return (density, diagonal)


def solution(mesh):
    in_specs = (
        P("pole", None, "row", None, "col", None),
        P("pole", None, ("row", "col"), None),
        P(("row", "col"), None),
        P(),
        P("pole", None, None, None),
        P("pole", None),
    )
    out_specs = (P("col", "row"), P())
    return jax.shard_map(
        per_device, mesh=mesh, in_specs=in_specs, out_specs=out_specs, check_vma=False
    )
```

profile of v0, /device:TPU:2, one launch (start us, length us, event | category | flops | bytes accessed | tf_op | source)
XLA Modules:
  0.0 457.6 jit_solution(11535285280863356408)
XLA Ops:
  7.2 0.0 all-gather.3.cloned.1.call-start
  7.2 0.7 compare_bitcast_fusion
  7.9 0.7 fusion.25
  8.6 1.7 bitcast_select_fusion
  10.3 0.0 all-gather.3.cloned.1.call-update
  10.3 0.0 all-gather.5.cloned.1.call-start
  10.3 0.7 all-gather.5.cloned.1.call-update
  11.1 0.0 reduce-scatter.2.cloned.1.call-start
  11.1 1.4 fusion.28
  12.5 3.8 fusion.26
  16.3 38.6 %all-gather.3.cloned.1.call-done = bf16[2,1024,512]{2,1,0:T(8,128)(2,1)} async-done(((bf16[2,128,512]{2,1,0:T(8,128)(2,1)}), bf16[2,1024,512]{2,1,0:T(8,128)(2,1)}) %all-gather.3.cloned.1.call-update) | async-done | bytes 2097168 | tf_op jit(solution)/shard_map/all_gather | solution.py:28
  54.9 0.0 copy-start.3
  54.9 2.7 fusion.2
  57.6 0.0 copy-done.3
  57.6 0.0 copy-start.2
  57.6 1.3 fusion
  58.9 0.3 copy-done.2
  59.2 1.3 fusion.12
  60.5 4.6 %multiply_subtract_fusion = (f32[512,1024]{1,0:T(8,128)}, f32[512,1024]{1,0:T(8,128)}) fusion(f32[512,1024]{1,0:T(8,128)S(1)} %fusion.12, f32[]{:T(128)} %bitcast.7, f32[]{:T(128)} %bitcast, f32[512,1024]{1,0:T(8,128)S(1)} %fusion, bf16[128,8,8,128]{3,2,1,0:T(8,128)(2,1)S(1)} %bitcast.67, bf16[2,1024,512]{2,1,0:T(8,128)(2,1)S(1)} %copy-done.3), kind=kOutput, calls=%fused_computation.8 | convolution fusion | flops 1076363264 | bytes 11534344 | tf_op jit(solution)/shard_map/jk,ij->ki/dot_general | solution.py:8
  65.1 0.0 copy-start.4
  65.1 0.0 reduce-scatter.2.cloned.1.call-update
  65.1 0.0 all-reduce.5.cloned.1.call-start
  65.2 0.9 copy-done.4
  66.1 1.3 subtract_multiply_fusion
  67.4 27.9 %all-gather.5.cloned.1.call-done = bf16[2,1024,512]{2,1,0:T(8,128)(2,1)} async-done(((bf16[2,128,512]{2,1,0:T(8,128)(2,1)}), bf16[2,1024,512]{2,1,0:T(8,128)(2,1)}) %all-gather.5.cloned.1.call-update) | async-done | bytes 2097168 | tf_op jit(solution)/shard_map/all_gather | solution.py:29
  95.3 2.7 fusion.27
  97.9 1.3 copy.8
  99.3 1.5 copy.9
  100.8 0.0 copy-start
  100.8 0.0 copy-start.1
  100.8 2.5 fusion.29
  103.3 0.0 copy-done
  103.3 0.0 copy-done.1
  103.3 1.2 fusion.30
  104.5 1.9 fusion.20
  106.4 2.5 fusion.19
  108.9 0.0 all-reduce.5.cloned.1.call-update
  108.9 0.0 all-reduce.3.cloned.1.call-start
  109.0 31.0 %reduce-scatter.2.cloned.1.call-done = f32[64,1024]{1,0:T(8,128)} async-done(((f32[512,1024]{1,0:T(8,128)}), f32[64,1024]{1,0:T(8,128)}) %reduce-scatter.2.cloned.1.call-update) | async-done | bytes 262160 | tf_op jit(solution)/shard_map/reduce_scatter | solution.py:37
  140.0 0.0 all-reduce.3.cloned.1.call-update
  140.1 259.7 %all-reduce.5.cloned.1.call-done = f32[512,128]{1,0:T(8,128)} async-done(((f32[512,128]{1,0:T(8,128)}), f32[512,128]{1,0:T(8,128)}) %all-reduce.5.cloned.1.call-update) | async-done | bytes 262160 | tf_op jit(solution)/shard_map/psum | solution.py:50
  399.8 48.0 %all-reduce.3.cloned.1.call-done = f32[64,1024]{1,0:T(8,128)} async-done(((f32[64,1024]{1,0:T(8,128)}), f32[64,1024]{1,0:T(8,128)}) %all-reduce.3.cloned.1.call-update) | async-done | bytes 262160 | tf_op jit(solution)/shard_map/psum | solution.py:38
  447.8 1.7 copy.36
  449.4 1.7 copy.37
Async XLA Ops:
  7.2 47.7 %all-gather.3.cloned.1.call-start = ((), (), s32[]{:S(2)}) async-start(), calls=%async_computation.1 | async-start | bytes 2359296 | tf_op jit(solution)/shard_map/all_gather | solution.py:28
  10.3 85.0 %all-gather.5.cloned.1.call-start = ((), (), s32[]{:S(2)}) async-start(), calls=%async_computation.4 | async-start | bytes 2359296 | tf_op jit(solution)/shard_map/all_gather | solution.py:29
  11.1 129.0 %reduce-scatter.2.cloned.1.call-start = ((), (), s32[]{:S(2)}) async-start(), calls=%async_computation.2 | async-start | bytes 2359296 | tf_op jit(solution)/shard_map/reduce_scatter | solution.py:37
  54.9 2.7 copy-start.3
  57.6 1.6 copy-start.2
  65.1 0.9 copy-start.4
  65.1 334.7 %all-reduce.5.cloned.1.call-start = ((), (), s32[]{:S(2)}) async-start(), calls=%async_computation.5 | async-start | bytes 524288 | tf_op jit(solution)/shard_map/psum | solution.py:50
  100.8 2.6 copy-start
  100.8 2.6 copy-start.1
  108.9 338.8 %all-reduce.3.cloned.1.call-start = ((), (), s32[]{:S(2)}) async-start(), calls=%async_computation.3 | async-start | bytes 524288 | tf_op jit(solution)/shard_map/psum | solution.py:38
Sparse Core Ops, SparseCore 0:
  10.4 44.4 all-gather.2
  57.3 37.9 all-gather.4
  97.8 42.1 reduce-scatter.1
  145.9 253.8 all-reduce.4
  402.0 45.7 all-reduce.2
where the time goes:
time: 458 us
  waiting for transfers between devices  406 us (89%)
  matrix products  18 us (4%)
  local copies, waits for them, and re-layouts  15.2 us (3%)
  between operations  13.9 us (3%)
    psum x1, waiting for transfers between devices, per_device(): lax.psum(local_term.reshape(total_cols, slot_width), ('pole', 'row', 'col'))  260 us
    psum x1, waiting for transfers between devices, per_device(): density = lax.psum(part, 'pole')  48 us
    all_gather x1, waiting for transfers between devices, per_device(): column_rows = lax.all_gather(masked, 'row', axis=1, tiled=True)  38.6 us
    reduce_scatter x1, waiting for transfers between devices, per_device(): part = lax.psum_scatter(weighted, 'col', scatter_dimension=0, tiled=True)  31 us
    all_gather x1, waiting for transfers between devices, per_device(): own_rows = lax.all_gather(masked, 'col', axis=1, tiled=True)  27.9 us
    dot_general x4, matrix products, contract(): jnp.einsum('jk,ij->ki', left, right, preferred_element_type=jnp.float32)  9.92 us
  transfers between devices with their start and end apart: 5, of which 5 were waited for; matrix products, arithmetic and copies ran while one was open for 7% of the time, Pallas kernels for 0%

commit v1 on v0

--- a/solution.py
+++ b/solution.py
@@ -25,7 +25,10 @@
     masked = jnp.where(
         (column_ok & block_ok)[None, None, :], l_panel[0], jnp.zeros((), jnp.bfloat16)
     )
-    column_rows = lax.all_gather(masked, "row", axis=1, tiled=True)
+    size = lax.axis_size("row")
+    pieces = jnp.stack([masked for _ in range(size)])
+    pieces = lax.all_to_all(pieces, "row", split_axis=0, concat_axis=0)
+    column_rows = jnp.concatenate(pieces, axis=1)
     own_rows = lax.all_gather(masked, "col", axis=1, tiled=True)
     local_rows = found_inverse.shape[2]
     inverse = found_inverse[0].reshape(2, local_rows, row_count * slot_width)

time: 458 us -> 433 us (0.945)
  waiting for transfers between devices: 406 us -> 373 us
  starting transfers between devices: 0.2 us -> 6.62 us
    all_gather x1 -> x0, waiting for transfers between devices: 38.6 us -> none  [per_device(): column_rows = lax.all_gather(masked, 'row', axis=1, tiled=True)]
    all_to_all x0 -> x1, waiting for transfers between devices: none -> 30.2 us  [per_device(): pieces = lax.all_to_all(pieces, 'row', split_axis=0, concat_axis=0)]
    all_gather x1, waiting for transfers between devices: 27.9 us -> 0.02 us  [per_device(): own_rows = lax.all_gather(masked, 'col', axis=1, tiled=True)]
    all_to_all x0 -> x1, starting transfers between devices: none -> 6.32 us  [per_device(): pieces = lax.all_to_all(pieces, 'row', split_axis=0, concat_axis=0)]
  transfers between devices with their start and end apart: 5 -> 5, of which waited for: 5 -> 4; matrix products, arithmetic and copies ran while one was open for 7% -> 7% of each run, Pallas kernels for 0% -> 0%
where the time goes in v1:
time: 433 us; the launch traced here: 432 us
  waiting for transfers between devices  373 us (86%)
  local copies, waits for them, and re-layouts  18 us (4%)
  matrix products  16.7 us (4%)
  between operations  13.9 us (3%)
  starting transfers between devices  6.62 us (2%)
  other arithmetic  4.4 us (1%)
    psum x1, waiting for transfers between devices, per_device(): lax.psum(local_term.reshape(total_cols, slot_width), ('pole', 'row', 'col'))  260 us
    psum x1, waiting for transfers between devices, per_device(): density = lax.psum(part, 'pole')  48 us
    reduce_scatter x1, waiting for transfers between devices, per_device(): part = lax.psum_scatter(weighted, 'col', scatter_dimension=0, tiled=True)  34.4 us
    all_to_all x1, waiting for transfers between devices, per_device(): pieces = lax.all_to_all(pieces, 'row', split_axis=0, concat_axis=0)  30.2 us
  transfers between devices with their start and end apart: 5, of which 4 were waited for; matrix products, arithmetic and copies ran while one was open for 7% of the time, Pallas kernels for 0%

profile of v1, /device:TPU:2, one launch (start us, length us, event | category | flops | bytes accessed | tf_op | source)
XLA Modules:
  0.0 432.3 jit_solution(3155090668460693979)
XLA Ops:
  7.2 0.7 compare_bitcast_fusion
  7.8 0.7 fusion.25
  8.6 1.0 select_bitcast_fusion
  9.5 1.5 stack.5
  11.1 0.0 copy-start.4
  11.1 0.0 copy-start.6
  11.1 6.3 %all-to-all-start = ((bf16[8,2,128,512]{3,2,1,0:T(8,128)(2,1)}), bf16[8,2,128,512]{3,2,1,0:T(8,128)(2,1)S(1)}, u32[]{:S(2)}, u32[]{:S(2)}) async-start(bf16[8,2,128,512]{3,2,1,0:T(8,128)(2,1)} %stack.5), calls=%async_computation | async-start | bytes 4194304 | tf_op jit(solution)/shard_map/all_to_all | solution.py:30
  17.4 0.0 all-gather.2.cloned.1.call-start
  17.4 0.0 copy-done.4
  17.4 0.7 bitcast_select_fusion
  18.1 0.0 all-gather.2.cloned.1.call-update
  18.1 0.0 reduce-scatter.2.cloned.1.call-start
  18.2 0.0 copy-done.6
  18.2 0.6 fusion.29
  18.8 4.5 %fusion.26 = (bf16[1,1,1024,8,1,128]{5,3,4,2,1,0:T(8,128)(2,1)}, bf16[1,1,1024,8,1,128]{5,3,4,2,1,0:T(8,128)(2,1)}) fusion(bf16[1,2,1024,8,1,128]{5,3,4,2,1,0:T(8,128)(2,1)} %param.6), kind=kLoop, calls=%fused_computation.32 | loop fusion | bytes 8388608 | tf_op jit(solution)/shard_map/slice | solution.py:35
  23.3 30.2 %all-to-all-done = bf16[8,2,128,512]{3,2,1,0:T(8,128)(2,1)S(1)} async-done(((bf16[8,2,128,512]{3,2,1,0:T(8,128)(2,1)}), bf16[8,2,128,512]{3,2,1,0:T(8,128)(2,1)S(1)}, u32[]{:S(2)}, u32[]{:S(2)}) %all-to-all-start) | async-done | bytes 2097184 | tf_op jit(solution)/shard_map/all_to_all | solution.py:30
  53.4 0.2 fusion.28
  53.6 1.4 copy-done.3
  55.0 1.3 fusion.2
  56.3 0.0 copy-start.2
  56.3 1.3 fusion
  57.6 0.3 copy-done.2
  58.0 1.3 fusion.12
  59.3 4.7 %multiply_subtract_fusion = (f32[512,1024]{1,0:T(8,128)}, f32[512,1024]{1,0:T(8,128)}) fusion(f32[512,1024]{1,0:T(8,128)S(1)} %fusion.12, f32[]{:T(128)} %bitcast.8, f32[]{:T(128)} %bitcast, f32[512,1024]{1,0:T(8,128)S(1)} %fusion, bf16[1024,512]{1,0:T(8,128)(2,1)S(1)} %bitcast.69, bf16[128,8,8,128]{3,2,1,0:T(8,128)(2,1)S(1)} %bitcast.67), kind=kOutput, calls=%fused_computation.8 | convolution fusion | flops 1076363264 | bytes 11534344 | tf_op jit(solution)/shard_map/jk,ij->ki/dot_general | solution.py:8
  64.0 0.0 reduce-scatter.2.cloned.1.call-update
  64.0 0.2 all-reduce.5.cloned.1.call-start
  64.2 0.7 copy-done.5
  64.9 1.3 subtract_multiply_fusion
  66.3 0.0 all-gather.2.cloned.1.call-done
  66.3 2.7 fusion.27
  69.0 1.3 copy.8
  70.3 1.5 copy.9
  71.8 0.0 copy-start
  71.8 0.0 copy-start.1
  71.8 2.5 fusion.30
  74.3 0.0 copy-done
  74.3 0.0 copy-done.1
  74.4 1.2 fusion.31
  75.5 1.9 fusion.20
  77.4 2.5 fusion.19
  79.9 0.0 all-reduce.5.cloned.1.call-update
  80.0 0.0 all-reduce.3.cloned.1.call-start
  80.0 34.4 %reduce-scatter.2.cloned.1.call-done = f32[64,1024]{1,0:T(8,128)} async-done(((f32[512,1024]{1,0:T(8,128)}), f32[64,1024]{1,0:T(8,128)}) %reduce-scatter.2.cloned.1.call-update) | async-done | bytes 262160 | tf_op jit(solution)/shard_map/reduce_scatter | solution.py:40
  114.4 0.0 all-reduce.3.cloned.1.call-update
  114.5 259.9 %all-reduce.5.cloned.1.call-done = f32[512,128]{1,0:T(8,128)} async-done(((f32[512,128]{1,0:T(8,128)}), f32[512,128]{1,0:T(8,128)}) %all-reduce.5.cloned.1.call-update) | async-done | bytes 262160 | tf_op jit(solution)/shard_map/psum | solution.py:53
  374.4 48.0 %all-reduce.3.cloned.1.call-done = f32[64,1024]{1,0:T(8,128)} async-done(((f32[64,1024]{1,0:T(8,128)}), f32[64,1024]{1,0:T(8,128)}) %all-reduce.3.cloned.1.call-update) | async-done | bytes 262160 | tf_op jit(solution)/shard_map/psum | solution.py:41
  422.4 1.7 copy.36
  424.1 1.7 copy.37
  (2 shorter events, 0.0 us)
Async XLA Ops:
  11.1 6.3 %copy-start.4 = (bf16[1,2,128,512]{3,2,1,0:T(8,128)(2,1)S(1)}, bf16[1,2,128,512]{3,2,1,0:T(8,128)(2,1)}, u32[]{:S(2)}) copy-start(bf16[1,2,128,512]{3,2,1,0:T(8,128)(2,1)} %param.7) | copy-start | bytes 786436
  11.1 7.1 %copy-start.6 = (f32[1,2]{1,0:T(1,128)S(1)}, f32[1,2]{1,0:T(1,128)}, u32[]{:S(2)}) copy-start(f32[1,2]{1,0:T(1,128)} %param.11) | copy-start | bytes 28
  11.1 42.4 %all-to-all-start = ((bf16[8,2,128,512]{3,2,1,0:T(8,128)(2,1)}), bf16[8,2,128,512]{3,2,1,0:T(8,128)(2,1)S(1)}, u32[]{:S(2)}, u32[]{:S(2)}) async-start(bf16[8,2,128,512]{3,2,1,0:T(8,128)(2,1)} %stack.5), calls=%async_computation | async-start | bytes 4194304 | tf_op jit(solution)/shard_map/all_to_all | solution.py:30
  17.4 48.9 %all-gather.2.cloned.1.call-start = ((), (), s32[]{:S(2)}) async-start(), calls=%async_computation.4 | async-start | bytes 2359296 | tf_op jit(solution)/shard_map/all_gather | solution.py:32
  18.1 96.3 %reduce-scatter.2.cloned.1.call-start = ((), (), s32[]{:S(2)}) async-start(), calls=%async_computation.2 | async-start | bytes 2359296 | tf_op jit(solution)/shard_map/reduce_scatter | solution.py:40
  53.4 1.6 copy-start.3
  56.3 1.6 copy-start.2
  64.0 0.9 copy-start.5
  64.0 310.4 %all-reduce.5.cloned.1.call-start = ((), (), s32[]{:S(2)}) async-start(), calls=%async_computation.5 | async-start | bytes 524288 | tf_op jit(solution)/shard_map/psum | solution.py:53
  71.8 2.6 copy-start
  71.8 2.6 copy-start.1
  80.0 342.5 %all-reduce.3.cloned.1.call-start = ((), (), s32[]{:S(2)}) async-start(), calls=%async_computation.3 | async-start | bytes 524288 | tf_op jit(solution)/shard_map/psum | solution.py:41
Sparse Core Ops, SparseCore 0:
  20.6 43.3 all-gather.1
  66.6 47.8 reduce-scatter.1
  120.5 253.8 all-reduce.4
  376.6 45.7 all-reduce.2
